TPU v7x, 512 devices: a whole 4x4x16 slice. The times are simulated.
512 devices in a mesh: tm: 32 (over x, z_lo), height: 8 (over z_hi, y), dp: 2 (over core).
Axes of the slice: x: 4, y: 4, z: 16 (z_hi: 2, z_lo: 8; z = z_hi * 8 + z_lo), core: 2. Of those that a mesh axis runs over, the one named last changes fastest.
Arguments:
- frames_in: bfloat16 [2, 128, 32, 48, 256], P('dp', 'tm', 'height'), may hold values from -6 to 6
- cotangent: bfloat16 [2, 128, 32, 48, 256], P('dp', 'tm', 'height'), may hold values from -6 to 6
- w_spatial: bfloat16 [3, 3, 256, 256], replicated, may hold values from -0.125 to 0.125
- w_temporal: bfloat16 [3, 256, 256], replicated, may hold values from -0.21875 to 0.21875
Outputs:
- decoded: bfloat16 [2, 128, 32, 48, 256], P('dp', 'tm', 'height')
- input_grad: bfloat16 [2, 128, 32, 48, 256], P('dp', 'tm', 'height')
- spatial_grad: bfloat16 [3, 3, 256, 256], replicated
- temporal_grad: bfloat16 [3, 256, 256], replicated
All inputs are finite; a program needn't handle non-finite values.
Results may differ from a plain program's by a relative error of at most 0.0061.
Values may be sent and summed in bfloat16 or wider, within the bound.
No kernel may reach another device: no remote copies, remote signals or barrier semaphores. Data moves between devices by JAX's collectives and lax.ppermute only.
A program may use at most 64 MiB of HBM per device.

v0:
```python
import math
import jax
import jax.numpy as jnp
from jax import lax
from jax.sharding import PartitionSpec as P


def extended(x, sides, width):
    for axis, dim in sides:
        count, length = (lax.axis_size(axis), x.shape[dim])
        up = [(i, (i + 1) % count) for i in range(count - 1)]
        down = [(j, i) for i, j in up]
        last = lax.slice_in_dim(x, length - width, length, axis=dim)
        initial = lax.slice_in_dim(x, 0, width, axis=dim)
        before = lax.ppermute(last, axis, up)
        after = lax.ppermute(initial, axis, down)
        x = jnp.concatenate([before, x, after], axis=dim)
    return x


def from_behind(block, axis, distance):
    devices = range(lax.axis_size(axis))
    route = [(i - distance, i) for i in devices if i - distance in devices]
    return lax.ppermute(block, axis, route)


def silu_slope(values):
    sigmoid_value = jax.nn.sigmoid(values)
    return sigmoid_value * (1.0 + values * (1.0 - sigmoid_value))


def frame_taps(source, frame_count):
    return jnp.concatenate(
        [source[shift_tap : shift_tap + frame_count] for shift_tap in range(3)], axis=-1
    )


def flat_dot(left_side, right_side):
    return jnp.dot(
        left_side.reshape(-1, left_side.shape[-1]), right_side, preferred_element_type=jnp.float32
    )


def local(frames_in, cotangent, w_spatial, w_temporal):
    inputs = frames_in[0]
    upstream = cotangent[0]
    frame_count, row_count, col_count, channels = inputs.shape
    temporal_flat = w_temporal.reshape(3 * channels, channels)
    temporal_back = jnp.concatenate([w_temporal[2].T, w_temporal[1].T, w_temporal[0].T], axis=0)
    first_shard = lax.axis_index("tm") == 0
    activated = jax.nn.silu(inputs.astype(jnp.float32)).astype(jnp.bfloat16)
    activ_rows = extended(activated, (("height", 1),), 1)
    activ_pad = jnp.pad(activ_rows, ((0, 0), (0, 0), (1, 1), (0, 0)))
    spatial_out = lax.conv_general_dilated(
        activ_pad,
        w_spatial,
        (1, 1),
        "VALID",
        dimension_numbers=("NHWC", "HWIO", "NHWC"),
        preferred_element_type=jnp.float32,
    ).astype(jnp.bfloat16)
    earlier = from_behind(spatial_out[frame_count - 2 :], "tm", 1)
    repeated = jnp.broadcast_to(spatial_out[:1], earlier.shape)
    earlier = jnp.where(first_shard, repeated, earlier)
    padded_frames = jnp.concatenate([earlier, spatial_out], axis=0)
    frame_stack = frame_taps(padded_frames, frame_count).reshape(-1, 3 * channels)
    temporal_out = jnp.dot(frame_stack, temporal_flat, preferred_element_type=jnp.float32).reshape(
        inputs.shape
    )
    decoded = (inputs.astype(jnp.float32) + temporal_out).astype(jnp.bfloat16)
    upstream_ext = jnp.pad(upstream, ((2, 2), (0, 0), (0, 0), (0, 0)))
    frame_part = flat_dot(frame_taps(upstream_ext, frame_count + 2), temporal_back)
    frame_part = frame_part.reshape(frame_count + 2, row_count, col_count, channels)
    rim_part = frame_part[:2]
    returned = from_behind(rim_part, "tm", -1)
    frame_sum = frame_part[2:]
    frame_sum = frame_sum.at[frame_count - 2 :].add(returned)
    frame_sum = frame_sum.at[0].add(jnp.where(first_shard, rim_part[0] + rim_part[1], 0.0))
    frame_grad = frame_sum.astype(jnp.bfloat16)
    grad_pad = jnp.pad(frame_grad, ((0, 0), (2, 2), (1, 1), (0, 0)))
    spatial_flip = jnp.flip(w_spatial, (0, 1)).transpose(0, 1, 3, 2)
    grad_ext = lax.conv_general_dilated(
        grad_pad,
        spatial_flip,
        (1, 1),
        "VALID",
        dimension_numbers=("NHWC", "HWIO", "NHWC"),
        preferred_element_type=jnp.float32,
    )
    edge_rows = jnp.stack([grad_ext[:, 0], grad_ext[:, row_count + 1]], axis=1)
    arrived = extended(edge_rows.astype(jnp.bfloat16), (("height", 1),), 1).astype(edge_rows.dtype)
    act_grad = grad_ext[:, 1 : row_count + 1]
    act_grad = act_grad.at[:, 0].add(arrived[:, 0])
    act_grad = act_grad.at[:, row_count - 1].add(arrived[:, 3])
    input_grad = (
        upstream.astype(jnp.float32) + silu_slope(inputs.astype(jnp.float32)) * act_grad
    ).astype(jnp.bfloat16)
    cell_count = (
        frame_count
        * lax.axis_size("tm")
        * row_count
        * lax.axis_size("height")
        * col_count
        * lax.axis_size("dp")
    )
    grad_scale = 1.0 / math.sqrt(cell_count)
    contract = (((0,), (0,)), ((), ()))
    spatial_term = lax.conv_general_dilated(
        activ_pad,
        frame_grad,
        (1, 1),
        "VALID",
        dimension_numbers=("CHWN", "IHWO", "HWNC"),
        preferred_element_type=jnp.float32,
    ).reshape(9 * channels, channels)
    temporal_term = lax.dot_general(
        frame_stack, upstream.reshape(-1, channels), contract, preferred_element_type=jnp.float32
    )
    weight_terms = jnp.concatenate([spatial_term, temporal_term], axis=0) * grad_scale
    summed = lax.psum(weight_terms, ("tm", "height", "dp")).astype(jnp.bfloat16)
    spatial_grad = summed[: 9 * channels].reshape(3, 3, channels, channels)
    temporal_grad = summed[9 * channels :].reshape(3, channels, channels)
    return (decoded[None], input_grad[None], spatial_grad, temporal_grad)


def solution(mesh):
    return jax.shard_map(
        local,
        mesh=mesh,
        in_specs=(
            P("dp", "tm", "height", None, None),
            P("dp", "tm", "height", None, None),
            P(),
            P(),
        ),
        out_specs=(
            P("dp", "tm", "height", None, None),
            P("dp", "tm", "height", None, None),
            P(),
            P(),
        ),
        check_vma=False,
    )
```

profile of v0, /device:TPU:32, one launch (start us, length us, event | category | flops | bytes accessed | tf_op | source)
XLA Modules:
  0.0 292.8 jit_solution(13264414294264656128)
XLA Ops:
  0.6 1.2 slice_bitcast_fusion.2
  1.8 1.5 pad_slice_fusion.2
  5.3 7.4 %collective-permute-start.3 = (f32[2,4,48,256]{3,0,2,1:T(2,128)}, f32[2,4,48,256]{3,0,2,1:T(2,128)}, u32[]{:S(2)}, u32[]{:S(2)}) collective-permute-start(f32[2,4,48,256]{3,0,2,1:T(2,128)} %copy.24), channel_id=1, source_target_pairs={{16,0},{32,16},{48,32},{64,48},{80,64},{96,80},{112,96},{128,112},... | collective-permute-start | bytes 1179656 | tf_op jit(solution)/shard_map/ppermute | solution.py:24
  13.6 1.6 copy.26
  15.3 3.2 %collective-permute-done.3 = f32[2,4,48,256]{3,0,2,1:T(2,128)} collective-permute-done((f32[2,4,48,256]{3,0,2,1:T(2,128)}, f32[2,4,48,256]{3,0,2,1:T(2,128)}, u32[]{:S(2)}, u32[]{:S(2)}) %collective-permute-start.3) | collective-permute-done | bytes 393248 | tf_op jit(solution)/shard_map/ppermute | solution.py:24
  18.5 1.5 fusion.34
  20.3 6.3 %scatter-add.15 = f32[4,4,48,256]{3,0,2,1:T(4,128)S(1)} dynamic-update-slice(f32[4,4,48,256]{3,0,2,1:T(4,128)S(1)} %fusion.34, f32[1,4,48,256]{3,0,2,1:T(1,128)S(1)} %slice_add_fusion.2, s32[]{:T(128)} %constant.118.clone.1, s32[]{:T(128)} %constant.118.clone.1, s32[]{:T(128)} %constant.118.clone.1, s32[]{:T(128)} %constant.118.clone.1) | dynamic-update-slice | bytes 393220 | tf_op jit(solution)/shard_map/scatter-add | solution.py:78
  27.1 1.8 fusion.50
  31.3 4.1 %collective-permute-start.4 = (bf16[4,1,48,256]{3,2,1,0:T(8,128)(2,1)S(1)}, bf16[4,1,48,256]{3,2,1,0:T(8,128)(2,1)}, u32[]{:S(2)}, u32[]{:S(2)}) collective-permute-start(bf16[4,1,48,256]{3,2,1,0:T(8,128)(2,1)S(1)} %slice_bitcast_fusion.4), channel_id=1, source_target_pairs={{0,2},{2,4},{4,6},{6,8},{8,10},{10,12},{12,14},{1,3},{3,5},{5,7},{... | collective-permute-start | bytes 294920 | tf_op jit(solution)/shard_map/ppermute | solution.py:15
  35.4 1.6 copy.35
  38.0 1.3 collective-permute-start.5
  40.7 3.8 %collective-permute-done.5 = bf16[4,1,48,256]{3,2,1,0:T(8,128)(2,1)S(1)} collective-permute-done((bf16[4,1,48,256]{3,2,1,0:T(8,128)(2,1)S(1)}, bf16[4,1,48,256]{3,2,1,0:T(8,128)(2,1)S(1)}, u32[]{:S(2)}, u32[]{:S(2)}) %collective-permute-start.5) | collective-permute-done | bytes 98336 | tf_op jit(solution)/shard_map/ppermute | solution.py:16
  45.5 1.1 fusion.35
  46.6 2.9 collective-permute-start
  49.5 1.3 collective-permute-start.1
  51.7 14.0 %collective-permute-done.1 = bf16[4,1,48,256]{3,2,1,0:T(8,128)(2,1)S(1)} collective-permute-done((bf16[4,1,48,256]{3,2,1,0:T(8,128)(2,1)S(1)}, bf16[4,1,48,256]{3,2,1,0:T(8,128)(2,1)S(1)}, u32[]{:S(2)}, u32[]{:S(2)}) %collective-permute-start.1) | collective-permute-done | bytes 98336 | tf_op jit(solution)/shard_map/ppermute | solution.py:16
  66.9 1.2 fusion.1
  68.7 3.1 %collective-permute-start.2 = (bf16[2,4,48,256]{3,2,1,0:T(8,128)(2,1)S(1)}, bf16[2,4,48,256]{3,2,1,0:T(8,128)(2,1)S(1)}, u32[]{:S(2)}, u32[]{:S(2)}) collective-permute-start(bf16[2,4,48,256]{3,2,1,0:T(8,128)(2,1)S(1)} %slice.241), channel_id=1, source_target_pairs={{0,16},{16,32},{32,48},{48,64},{64,80},{80,96},{96,112},{112,128},... | collective-permute-start | bytes 589832 | tf_op jit(solution)/shard_map/ppermute | solution.py:24
  71.9 2.1 fusion.25
  74.0 2.3 collective-permute-done.2
  77.1 2.0 maximum_multiply_fusion
  79.1 210.6 %all-reduce.2 = bf16[3072,256]{1,0:T(8,128)(2,1)S(1)} all-reduce(f32[3072,256]{1,0:T(8,128)} %maximum_multiply_fusion), channel_id=1, replica_groups=mesh['tm'=32,'height'=8,'dp'=2] {'tm','height','dp'}, use_global_device_ids=true, to_apply=%region_0.1 | all-reduce | flops 786432 | bytes 4718592 | tf_op jit(solution)/shard_map/psum | solution.py:120
  290.5 1.1 slice.260
  291.6 1.2 fusion.3
  (62 shorter events, 13.4 us)
Async XLA Ops:
  0.6 26.5 %copy-start = (bf16[3,3,256,256]{3,2,1,0:T(8,128)(2,1)S(1)}, bf16[3,3,256,256]{3,2,1,0:T(8,128)(2,1)}, u32[]{:S(2)}) copy-start(bf16[3,3,256,256]{3,2,1,0:T(8,128)(2,1)} %param.14) | copy-start | bytes 3538948
  5.3 13.2 %collective-permute-start.3 = (f32[2,4,48,256]{3,0,2,1:T(2,128)}, f32[2,4,48,256]{3,0,2,1:T(2,128)}, u32[]{:S(2)}, u32[]{:S(2)}) collective-permute-start(f32[2,4,48,256]{3,0,2,1:T(2,128)} %copy.24), channel_id=1, source_target_pairs={{16,0},{32,16},{48,32},{64,48},{80,64},{96,80},{112,96},{128,112},... | collective-permute-start | bytes 1179656 | tf_op jit(solution)/shard_map/ppermute | solution.py:24
  20.3 6.8 %copy-start.7 = (pred[32,7]{0,1:T(8,128)(4,1)S(1)}, pred[32,7]{0,1:T(8,128)(4,1)}, u32[]{:S(2)}) copy-start(pred[32,7]{0,1:T(8,128)(4,1)} %constant.137) | copy-start | bytes 676
  31.3 9.4 %collective-permute-start.4 = (bf16[4,1,48,256]{3,2,1,0:T(8,128)(2,1)S(1)}, bf16[4,1,48,256]{3,2,1,0:T(8,128)(2,1)}, u32[]{:S(2)}, u32[]{:S(2)}) collective-permute-start(bf16[4,1,48,256]{3,2,1,0:T(8,128)(2,1)S(1)} %slice_bitcast_fusion.4), channel_id=1, source_target_pairs={{0,2},{2,4},{4,6},{6,8},{8,10},{10,12},{12,14},{1,3},{3,5},{5,7},{... | collective-permute-start | bytes 294920 | tf_op jit(solution)/shard_map/ppermute | solution.py:15
  38.0 6.5 %collective-permute-start.5 = (bf16[4,1,48,256]{3,2,1,0:T(8,128)(2,1)S(1)}, bf16[4,1,48,256]{3,2,1,0:T(8,128)(2,1)S(1)}, u32[]{:S(2)}, u32[]{:S(2)}) collective-permute-start(bf16[4,1,48,256]{3,2,1,0:T(8,128)(2,1)S(1)} %slice_bitcast_fusion.3), channel_id=1, source_target_pairs={{2,0},{4,2},{6,4},{8,6},{10,8},{12,10},{14,12},{3,1},{5,3},{7,5},{... | collective-permute-start | bytes 294920 | tf_op jit(solution)/shard_map/ppermute | solution.py:16
  40.1 5.3 %copy-start.1 = (bf16[1,4,4,48,256]{4,3,2,1,0:T(8,128)(2,1)S(1)}, bf16[1,4,4,48,256]{4,3,2,1,0:T(8,128)(2,1)}, u32[]{:S(2)}) copy-start(bf16[1,4,4,48,256]{4,3,2,1,0:T(8,128)(2,1)} %param.13) | copy-start | bytes 1179652
  40.2 5.3 %copy-start.4 = (bf16[1,4,4,48,256]{4,3,2,1,0:T(8,128)(2,1)S(1)}, bf16[1,4,4,48,256]{4,3,2,1,0:T(8,128)(2,1)}, u32[]{:S(2)}) copy-start(bf16[1,4,4,48,256]{4,3,2,1,0:T(8,128)(2,1)} %param.12) | copy-start | bytes 1179652
  46.6 5.1 %collective-permute-start = (bf16[4,1,48,256]{3,2,1,0:T(8,128)(2,1)S(1)}, bf16[4,1,48,256]{3,2,1,0:T(8,128)(2,1)S(1)}, u32[]{:S(2)}, u32[]{:S(2)}) collective-permute-start(bf16[4,1,48,256]{3,2,1,0:T(8,128)(2,1)S(1)} %get-tuple-element.66), channel_id=1, source_target_pairs={{0,2},{2,4},{4,6},{6,8},{8,10},{10,12},{12,14},{1,3},{3,5},{5,7},{... | collective-permute-start | bytes 294920 | tf_op jit(solution)/shard_map/ppermute | solution.py:15
  49.5 16.2 %collective-permute-start.1 = (bf16[4,1,48,256]{3,2,1,0:T(8,128)(2,1)S(1)}, bf16[4,1,48,256]{3,2,1,0:T(8,128)(2,1)S(1)}, u32[]{:S(2)}, u32[]{:S(2)}) collective-permute-start(bf16[4,1,48,256]{3,2,1,0:T(8,128)(2,1)S(1)} %get-tuple-element.67), channel_id=1, source_target_pairs={{2,0},{4,2},{6,4},{8,6},{10,8},{12,10},{14,12},{3,1},{5,3},{7,5},{... | collective-permute-start | bytes 294920 | tf_op jit(solution)/shard_map/ppermute | solution.py:16
  66.2 0.7 copy-start.8
  68.7 7.6 %collective-permute-start.2 = (bf16[2,4,48,256]{3,2,1,0:T(8,128)(2,1)S(1)}, bf16[2,4,48,256]{3,2,1,0:T(8,128)(2,1)S(1)}, u32[]{:S(2)}, u32[]{:S(2)}) collective-permute-start(bf16[2,4,48,256]{3,2,1,0:T(8,128)(2,1)S(1)} %slice.241), channel_id=1, source_target_pairs={{0,16},{16,32},{32,48},{48,64},{64,80},{80,96},{96,112},{112,128},... | collective-permute-start | bytes 589832 | tf_op jit(solution)/shard_map/ppermute | solution.py:24
  76.4 0.7 copy-start.2
  289.7 1.9 copy-start.3
  289.7 1.9 copy-start.5
  289.7 1.9 copy-start.6
where the time goes:
time: 293 us
  blocking collectives  211 us (72%)
  waiting for transfers between devices  24.2 us (8%)
  local copies, waits for them, and re-layouts  22.6 us (8%)
  starting transfers between devices  20 us (7%)
  matrix products  7.58 us (3%)
  other arithmetic  6.71 us (2%)
    psum x1, blocking collectives, local(): summed = lax.psum(weight_terms, ('tm', 'height', 'dp')).astype(jnp.bfloat16)  211 us
    ppermute x2, waiting for transfers between devices, extended(): after = lax.ppermute(initial, axis, down)  17.7 us
    ppermute x2, starting transfers between devices, from_behind(): return lax.ppermute(block, axis, route)  10.5 us
    ppermute x2, starting transfers between devices, extended(): before = lax.ppermute(last, axis, up)  6.98 us
    scatter-add x1, local copies, waits for them, and re-layouts, local(): frame_sum.at[0].add(jnp.where(first_shard, rim_part[0] + rim_part[1], 0.0))  6.33 us
  transfers between devices with their start and end apart: 6, of which 5 were waited for; matrix products, arithmetic and copies ran while one was open for 3% of the time, Pallas kernels for 0%

commit v1 on v0

--- a/solution.py
+++ b/solution.py
@@ -3,6 +3,8 @@
 import jax.numpy as jnp
 from jax import lax
 from jax.sharding import PartitionSpec as P
+
+_resolve_values = lambda xx: lax.psum(lax.psum(xx, axis_name="tm"), axis_name=("height", "dp"))
 
 
 def extended(x, sides, width):
@@ -117,7 +119,7 @@
         frame_stack, upstream.reshape(-1, channels), contract, preferred_element_type=jnp.float32
     )
     weight_terms = jnp.concatenate([spatial_term, temporal_term], axis=0) * grad_scale
-    summed = lax.psum(weight_terms, ("tm", "height", "dp")).astype(jnp.bfloat16)
+    summed = _resolve_values(weight_terms).astype(jnp.bfloat16)
     spatial_grad = summed[: 9 * channels].reshape(3, 3, channels, channels)
     temporal_grad = summed[9 * channels :].reshape(3, channels, channels)
     return (decoded[None], input_grad[None], spatial_grad, temporal_grad)

time: 293 us -> 780 us (2.66)
  the two profiles are of different devices: /device:TPU:32 before, /device:TPU:223 now
where the time goes in v1:
time: 780 us; the launch traced here: 779 us
  waiting for transfers between devices  490 us (63%)
  blocking collectives  218 us (28%)
  local copies, waits for them, and re-layouts  23.5 us (3%)
  starting transfers between devices  19.7 us (3%)
  between operations  14.5 us (2%)
    psum x1, waiting for transfers between devices, lax.psum(xx, axis_name='tm')  452 us
    psum x1, blocking collectives, lax.psum(lax.psum(xx, axis_name='tm'), axis_name=('height', 'dp'))  218 us
    ppermute x2, waiting for transfers between devices, extended(): after = lax.ppermute(initial, axis, down)  27.6 us
  transfers between devices with their start and end apart: 7, of which 6 were waited for; matrix products, arithmetic and copies ran while one was open for 1% of the time, Pallas kernels for 0%

profile of v1, /device:TPU:223, one launch (start us, length us, event | category | flops | bytes accessed | tf_op | source)
XLA Modules:
  0.0 779.3 jit_solution(16309484708782675760)
XLA Ops:
  7.2 1.1 slice_bitcast_fusion.2
  8.4 1.6 pad_slice_fusion.2
  11.9 1.9 collective-permute-start.3
  14.7 1.6 copy.26
  16.4 7.6 collective-permute-done.3
  24.1 1.5 fusion.34
  25.9 6.3 scatter-add.15
  32.7 1.8 fusion.50
  36.8 8.5 %collective-permute-start.4 = (bf16[4,1,48,256]{3,2,1,0:T(8,128)(2,1)S(1)}, bf16[4,1,48,256]{3,2,1,0:T(8,128)(2,1)}, u32[]{:S(2)}, u32[]{:S(2)}) collective-permute-start(bf16[4,1,48,256]{3,2,1,0:T(8,128)(2,1)S(1)} %slice_bitcast_fusion.4), channel_id=1, source_target_pairs={{0,2},{2,4},{4,6},{6,8},{8,10},{10,12},{12,14},{1,3},{3,5},{5,7},{... | collective-permute-start | bytes 294920 | tf_op jit(solution)/shard_map/ppermute | solution.py:17
  45.3 1.6 copy.35
  47.9 1.9 collective-permute-start.5
  51.3 13.9 %collective-permute-done.5 = bf16[4,1,48,256]{3,2,1,0:T(8,128)(2,1)S(1)} collective-permute-done((bf16[4,1,48,256]{3,2,1,0:T(8,128)(2,1)S(1)}, bf16[4,1,48,256]{3,2,1,0:T(8,128)(2,1)S(1)}, u32[]{:S(2)}, u32[]{:S(2)}) %collective-permute-start.5) | collective-permute-done | bytes 98336 | tf_op jit(solution)/shard_map/ppermute | solution.py:18
  66.2 1.1 fusion.35
  67.3 1.9 collective-permute-start
  69.2 3.4 collective-permute-start.1
  72.7 13.7 %collective-permute-done.1 = bf16[4,1,48,256]{3,2,1,0:T(8,128)(2,1)S(1)} collective-permute-done((bf16[4,1,48,256]{3,2,1,0:T(8,128)(2,1)S(1)}, bf16[4,1,48,256]{3,2,1,0:T(8,128)(2,1)S(1)}, u32[]{:S(2)}, u32[]{:S(2)}) %collective-permute-start.1) | collective-permute-done | bytes 98336 | tf_op jit(solution)/shard_map/ppermute | solution.py:18
  87.7 1.2 fusion.1
  89.5 2.1 collective-permute-start.2
  91.6 2.0 fusion.25
  93.6 2.3 collective-permute-done.2
  96.6 2.0 maximum_multiply_fusion
  99.6 1.2 fusion.3
  100.8 452.0 %all-reduce.4.cloned.1.call-done = f32[3072,256]{1,0:T(8,128)} async-done(((f32[3072,256]{1,0:T(8,128)}), f32[3072,256]{1,0:T(8,128)}) %all-reduce.4.cloned.1.call-update) | async-done | bytes 3145744 | tf_op jit(solution)/shard_map/psum | solution.py:7
  552.8 217.8 %all-reduce.5 = bf16[3072,256]{1,0:T(8,128)(2,1)S(1)} all-reduce(f32[3072,256]{1,0:T(8,128)} %all-reduce.4.cloned.1.call-done), channel_id=1, replica_groups=mesh['tm'=32,'height'=8,'dp'=2] {'height','dp'}, use_global_device_ids=true, to_apply=%region_1.2 | all-reduce | flops 786432 | bytes 4718592 | tf_op jit(solution)/shard_map/psum | solution.py:7
  (59 shorter events, 14.6 us)
Async XLA Ops:
  7.2 25.5 %copy-start = (bf16[3,3,256,256]{3,2,1,0:T(8,128)(2,1)S(1)}, bf16[3,3,256,256]{3,2,1,0:T(8,128)(2,1)}, u32[]{:S(2)}) copy-start(bf16[3,3,256,256]{3,2,1,0:T(8,128)(2,1)} %param.14) | copy-start | bytes 3538948
  7.2 545.6 %all-reduce.4.cloned.1.call-start = ((), (), s32[]{:S(2)}) async-start(), calls=%async_computation | async-start | bytes 6291456 | tf_op jit(solution)/shard_map/psum | solution.py:7
  11.9 12.2 %collective-permute-start.3 = (f32[2,4,48,256]{3,0,2,1:T(2,128)}, f32[2,4,48,256]{3,0,2,1:T(2,128)}, u32[]{:S(2)}, u32[]{:S(2)}) collective-permute-start(f32[2,4,48,256]{3,0,2,1:T(2,128)} %copy.24), channel_id=1, source_target_pairs={{16,0},{32,16},{48,32},{64,48},{80,64},{96,80},{112,96},{128,112},... | collective-permute-start | bytes 1179656 | tf_op jit(solution)/shard_map/ppermute | solution.py:26
  25.9 6.8 copy-start.4
  36.8 14.4 %collective-permute-start.4 = (bf16[4,1,48,256]{3,2,1,0:T(8,128)(2,1)S(1)}, bf16[4,1,48,256]{3,2,1,0:T(8,128)(2,1)}, u32[]{:S(2)}, u32[]{:S(2)}) collective-permute-start(bf16[4,1,48,256]{3,2,1,0:T(8,128)(2,1)S(1)} %slice_bitcast_fusion.4), channel_id=1, source_target_pairs={{0,2},{2,4},{4,6},{6,8},{8,10},{10,12},{12,14},{1,3},{3,5},{5,7},{... | collective-permute-start | bytes 294920 | tf_op jit(solution)/shard_map/ppermute | solution.py:17
  47.9 17.2 %collective-permute-start.5 = (bf16[4,1,48,256]{3,2,1,0:T(8,128)(2,1)S(1)}, bf16[4,1,48,256]{3,2,1,0:T(8,128)(2,1)S(1)}, u32[]{:S(2)}, u32[]{:S(2)}) collective-permute-start(bf16[4,1,48,256]{3,2,1,0:T(8,128)(2,1)S(1)} %slice_bitcast_fusion.3), channel_id=1, source_target_pairs={{2,0},{4,2},{6,4},{8,6},{10,8},{12,10},{14,12},{3,1},{5,3},{7,5},{... | collective-permute-start | bytes 294920 | tf_op jit(solution)/shard_map/ppermute | solution.py:18
  50.7 15.4 %copy-start.1 = (bf16[1,4,4,48,256]{4,3,2,1,0:T(8,128)(2,1)S(1)}, bf16[1,4,4,48,256]{4,3,2,1,0:T(8,128)(2,1)}, u32[]{:S(2)}) copy-start(bf16[1,4,4,48,256]{4,3,2,1,0:T(8,128)(2,1)} %param.13) | copy-start | bytes 1179652
  50.7 15.4 %copy-start.2 = (bf16[1,4,4,48,256]{4,3,2,1,0:T(8,128)(2,1)S(1)}, bf16[1,4,4,48,256]{4,3,2,1,0:T(8,128)(2,1)}, u32[]{:S(2)}) copy-start(bf16[1,4,4,48,256]{4,3,2,1,0:T(8,128)(2,1)} %param.12) | copy-start | bytes 1179652
  67.3 5.4 collective-permute-start
  69.2 17.2 %collective-permute-start.1 = (bf16[4,1,48,256]{3,2,1,0:T(8,128)(2,1)S(1)}, bf16[4,1,48,256]{3,2,1,0:T(8,128)(2,1)S(1)}, u32[]{:S(2)}, u32[]{:S(2)}) collective-permute-start(bf16[4,1,48,256]{3,2,1,0:T(8,128)(2,1)S(1)} %get-tuple-element.67), channel_id=1, source_target_pairs={{2,0},{4,2},{6,4},{8,6},{10,8},{12,10},{14,12},{3,1},{5,3},{7,5},{... | collective-permute-start | bytes 294920 | tf_op jit(solution)/shard_map/ppermute | solution.py:18
  86.9 0.7 copy-start.5
  89.5 6.4 collective-permute-start.2
  98.6 1.0 copy-start.3
Sparse Core Ops, SparseCore 0:
  98.7 454.0 all-reduce.3
